TPU v7x, 256 devices: a whole 4x4x8 slice. The times are simulated.
256 devices in a mesh: sub: 64 (over z, y, core), rhs: 4 (over x).
Axes of the slice: x: 4, y: 4, z: 8, core: 2. Of those that a mesh axis runs over, the one named last changes fastest.
Arguments:
- stiffness: float32 [3072, 4, 9216], P('sub'), may hold values from -1 to 2, as said below
- precond: float32 [3072, 9216], P('sub'), may hold values from -0.625 to 0.625
- rhs_vec: float32 [8, 294912], P('rhs', 'sub'), may hold values from -50 to 50
- cotangent: float32 [8, 294912], P('rhs', 'sub'), may hold values from -6 to 6
- col_index: int32 [3072, 4], P('sub'), may hold values from 0 to 59, as said below
- send_rows: int32 [64, 12], P('sub'), may hold values from 0 to 47, as said below
- counts: int32 [64], P('sub'), may hold values from 12 to 48, as said below
Outputs:
- solution: float32 [8, 294912], P('rhs', 'sub')
- grad_precond: float32 [3072, 9216], P('sub')
Inputs may be any that keep to these rules, and one draw needn't show every extreme that they name: `counts`: at least one subdomain has 48 live block rows. `send_rows`: for subdomain s, entries 0 to 5 are distinct live rows below counts[s] // 2 in increasing order, the first of them 0; entries 6 to 11 are distinct live rows from counts[s] // 2 on in increasing order, the last of them counts[s] - 1. Interface row j of the first group of subdomain s is coupled with interface row j of the second group of subdomain s - 1. `col_index`: index 6 + n is block n of the subdomain; indices below 6 and from 54 on are the blocks received from the previous and the next subdomain. Slot 0 of row n is 6 + n. A slot other than slot 0 that names 6 + n holds a zero block; rows that are not live hold only slot 0's block. `stiffness`: the operator A is symmetric and positive definite.
All inputs are finite; a program needn't handle non-finite values.
Results may differ from a plain program's by a relative error of at most 0.0003.
Values sent between devices are 32-bit elements; how exact they have to be, the bound alone decides.
A program may use at most 128 MiB of HBM per device.

v0:
```python
import jax
import jax.numpy as jnp
from jax import lax
from jax.sharding import PartitionSpec as P

BS = 96
K = 4
NBLK = 48
IF = 6
ITERS = 4
highest = lax.Precision.HIGHEST


def with_halo(array, sides, width):
    for axis, dim in sides:
        size, length = (lax.axis_size(axis), array.shape[dim])
        up = [(i, (i + 1) % size) for i in range(size - 1)]
        down = [(j, i) for i, j in up]
        last = lax.slice_in_dim(array, length - width, length, axis=dim)
        initial = lax.slice_in_dim(array, 0, width, axis=dim)
        before = lax.ppermute(last, axis, up)
        after = lax.ppermute(initial, axis, down)
        array = jnp.concatenate([before, array, after], axis=dim)
    return array


def local_dot(first_vec, second_vec):
    return jnp.sum(first_vec * second_vec, axis=(1, 2))


def widen(scalars):
    return scalars[:, None, None]


def precond_apply(weights, vector):
    projected = jnp.einsum("nab,rnb->rna", weights, vector, precision=highest)
    return (projected, vector + jnp.einsum("nab,rna->rnb", weights, projected, precision=highest))


def block_product(blocks, gathered):
    return jnp.einsum("nkab,rnkb->rna", blocks, gathered, precision=highest)


def stiff_apply(vector, blocks, columns, sending):
    outgoing = jnp.take(vector, sending, axis=1)
    framed = with_halo(outgoing, (("sub", 1),), IF)
    extended = jnp.concatenate([framed[:, :IF], vector, framed[:, 3 * IF :]], axis=1)
    return block_product(blocks, jnp.take(extended, columns, axis=1))


def norm_sum(first_vec, second_vec):
    return lax.psum(local_dot(first_vec, second_vec), "sub")


def grad_term(projected, zeta_bar, weight_zeta, resid_vec):
    first_part = jnp.einsum("rna,rnb->nab", projected, zeta_bar, precision=highest)
    return first_part + jnp.einsum("rna,rnb->nab", weight_zeta, resid_vec, precision=highest)


def shards(stiffness, precond, rhs_vec, cotangent, col_index, send_rows, counts):
    rhs_all, cot_all = (rhs_vec, cotangent)
    local_rhs = rhs_all.shape[0]
    blocks = stiffness.reshape(NBLK, K, BS, BS)
    weights = precond.reshape(NBLK, BS, BS)
    live_count = counts[0]
    sending = send_rows[0]
    live_mask = (jnp.arange(NBLK) < live_count).astype(jnp.float32)
    source = rhs_all.reshape(local_rhs, NBLK, BS) * live_mask[None, :, None]
    target = cot_all.reshape(local_rhs, NBLK, BS)
    residual = source
    first_proj, precon = precond_apply(weights, residual)
    first_res = residual
    direction = precon
    norm_now = norm_sum(residual, precon)
    solution = jnp.zeros_like(source)
    history = []
    for iteration in range(ITERS):
        applied = stiff_apply(direction, blocks, col_index, sending)
        curvature = lax.psum(local_dot(direction, applied), "sub")
        step_len = norm_now / curvature
        solution = solution + widen(step_len) * direction
        residual = residual - widen(step_len) * applied
        record = [direction, applied, step_len, curvature, norm_now]
        if iteration + 1 < ITERS:
            projected, precon = precond_apply(weights, residual)
            norm_next = norm_sum(residual, precon)
            ratio = norm_next / norm_now
            record = record + [residual, precon, projected, norm_next, ratio]
            direction = precon + widen(ratio) * direction
            norm_now = norm_next
        history.append(record)
    dir_bar = jnp.zeros_like(source)
    res_bar = jnp.zeros_like(source)
    norm_bar = jnp.zeros((local_rhs,), jnp.float32)
    grad_sum = jnp.zeros((NBLK, BS, BS), jnp.float32)
    for iteration in reversed(range(ITERS)):
        direction, applied, step_len, curvature, norm_now = history[iteration][:5]
        if iteration + 1 < ITERS:
            resid_next, precon, projected, norm_next, ratio = history[iteration][5:]
            ratio_bar, cot_dir = lax.psum(
                (local_dot(dir_bar, direction), local_dot(target, direction)), "sub"
            )
            norm_full = norm_bar + ratio_bar / norm_now
            zeta_bar = dir_bar + widen(norm_full) * resid_next
            weight_zeta, mapped = precond_apply(weights, zeta_bar)
            res_bar = res_bar + widen(norm_full) * precon + mapped
            res_image = lax.psum(local_dot(res_bar, applied), "sub")
            grad_sum = grad_sum + grad_term(projected, zeta_bar, weight_zeta, resid_next)
            dir_new = widen(ratio) * dir_bar
            norm_new = -ratio_bar * norm_next / (norm_now * norm_now)
        else:
            cot_dir = lax.psum(local_dot(target, direction), "sub")
            res_image = jnp.zeros_like(cot_dir)
            dir_new = jnp.zeros_like(source)
            norm_new = jnp.zeros_like(cot_dir)
        step_bar = cot_dir - res_image
        curv_bar = -step_bar * step_len / curvature
        dir_new = dir_new + widen(step_len) * target + widen(curv_bar) * applied
        image_bar = widen(curv_bar) * direction - widen(step_len) * res_bar
        dir_bar = dir_new + stiff_apply(image_bar, blocks, col_index, sending)
        norm_bar = norm_new + step_bar / curvature
    zeta_bar = dir_bar + widen(norm_bar) * first_res
    weight_zeta = jnp.einsum("nab,rnb->rna", weights, zeta_bar, precision=highest)
    grad_sum = grad_sum + grad_term(first_proj, zeta_bar, weight_zeta, first_res)
    grad_sum = lax.psum(grad_sum, "rhs")
    flat_solution = solution.reshape(local_rhs, NBLK * BS)
    return (flat_solution, grad_sum.reshape(NBLK, BS * BS))


def solution(mesh):
    in_specs = (
        P("sub", None, None),
        P("sub", None),
        P("rhs", "sub"),
        P("rhs", "sub"),
        P("sub", None),
        P("sub", None),
        P("sub"),
    )
    out_specs = (P("rhs", "sub"), P("sub", None))
    return jax.shard_map(shards, mesh=mesh, in_specs=in_specs, out_specs=out_specs, check_vma=False)
```

profile of v0, /device:TPU:1, one launch (start us, length us, event | category | flops | bytes accessed | tf_op | source)
XLA Modules:
  0.0 1994.4 jit_solution(11728397006781931206)
XLA Ops:
  10.1 2.2 reshape.53
  12.3 3.8 convolution_bitcast_fusion.22
  16.1 2.1 fusion.14
  18.9 4.6 collective-permute-start
  23.5 1.9 collective-permute-start.1
  25.8 10.6 reshape.54
  37.3 10.5 multiply_reduce_fusion.16
  47.8 127.8 %all-reduce.4 = (f32[2]{0:T(128)S(1)}, f32[2]{0:T(128)S(1)}) all-reduce(f32[2]{0:T(128)S(1)} %get-tuple-element.10, f32[2]{0:T(128)S(1)} %get-tuple-element.9), channel_id=1, replica_groups=mesh['sub'=64,'rhs'=4] {'sub'}, use_global_device_ids=true, to_apply=%region_1.0 | all-reduce | flops 4 | bytes 32 | tf_op jit(solution)/shard_map/psum | solution.py:52
  175.8 3.8 convolution_bitcast_fusion.20
  179.5 2.2 multiply_reduce_fusion.15
  181.7 127.4 %psum.135 = f32[2]{0:T(128)S(1)} all-reduce(f32[2]{0:T(128)S(1)} %get-tuple-element.44), channel_id=1, replica_groups=mesh['sub'=64,'rhs'=4] {'sub'}, use_global_device_ids=true, to_apply=%region_5.8 | all-reduce | flops 2 | bytes 16 | tf_op jit(solution)/shard_map/psum | solution.py:52
  309.9 1.9 collective-permute-start.2
  311.8 2.4 collective-permute-start.3
  314.3 2.5 collective-permute-done.3
  317.7 10.5 multiply_reduce_fusion.14
  328.2 122.2 %psum.136 = f32[2]{0:T(128)S(1)} all-reduce(f32[2]{0:T(128)S(1)} %get-tuple-element.46), channel_id=1, replica_groups=mesh['sub'=64,'rhs'=4] {'sub'}, use_global_device_ids=true, to_apply=%region_7.10 | all-reduce | flops 2 | bytes 16 | tf_op jit(solution)/shard_map/psum | solution.py:79
  450.5 3.8 convolution_bitcast_fusion.18
  454.2 2.2 multiply_reduce_fusion.13
  456.5 125.9 %psum.137 = f32[2]{0:T(128)S(1)} all-reduce(f32[2]{0:T(128)S(1)} %get-tuple-element.48), channel_id=1, replica_groups=mesh['sub'=64,'rhs'=4] {'sub'}, use_global_device_ids=true, to_apply=%region_9.12 | all-reduce | flops 2 | bytes 16 | tf_op jit(solution)/shard_map/psum | solution.py:52
  585.1 2.4 collective-permute-start.5
  587.5 2.5 collective-permute-done.5
  591.0 10.5 multiply_reduce_fusion.12
  601.5 122.2 %psum.138 = f32[2]{0:T(128)S(1)} all-reduce(f32[2]{0:T(128)S(1)} %get-tuple-element.50), channel_id=1, replica_groups=mesh['sub'=64,'rhs'=4] {'sub'}, use_global_device_ids=true, to_apply=%region_11.14 | all-reduce | flops 2 | bytes 16 | tf_op jit(solution)/shard_map/psum | solution.py:79
  723.8 3.8 convolution_bitcast_fusion.16
  727.6 2.2 multiply_reduce_fusion.11
  729.8 125.9 %psum.139 = f32[2]{0:T(128)S(1)} all-reduce(f32[2]{0:T(128)S(1)} %get-tuple-element.52), channel_id=1, replica_groups=mesh['sub'=64,'rhs'=4] {'sub'}, use_global_device_ids=true, to_apply=%region_13.16 | all-reduce | flops 2 | bytes 16 | tf_op jit(solution)/shard_map/psum | solution.py:52
  858.5 2.4 collective-permute-start.7
  861.0 2.4 collective-permute-done.7
  864.3 11.1 multiply_reduce_fusion.1
  875.5 122.0 %all-reduce.3 = (f32[2]{0:T(128)S(1)}, f32[2]{0:T(128)S(1)}) all-reduce(f32[2]{0:T(128)S(1)} %get-tuple-element.6, f32[2]{0:T(128)S(1)} %get-tuple-element.5), channel_id=1, replica_groups=mesh['sub'=64,'rhs'=4] {'sub'}, use_global_device_ids=true, to_apply=%region_15.18 | all-reduce | flops 4 | bytes 32 | tf_op jit(solution)/shard_map/psum | solution.py:79
  1000.7 4.2 collective-permute-start.9
  1006.6 10.5 multiply_reduce_fusion.8
  1017.1 123.4 %psum.142 = f32[2]{0:T(128)S(1)} all-reduce(f32[2]{0:T(128)S(1)} %get-tuple-element.55), channel_id=1, replica_groups=mesh['sub'=64,'rhs'=4] {'sub'}, use_global_device_ids=true, to_apply=%region_19.22 | all-reduce | flops 2 | bytes 16 | tf_op jit(solution)/shard_map/psum | solution.py:100
  1140.6 3.8 convolution_bitcast_fusion.14
  1144.4 2.2 multiply_reduce_fusion.6
  1146.6 5.2 fusion.64
  1151.9 124.5 %all-reduce.2 = (f32[2]{0:T(128)S(1)}, f32[2]{0:T(128)S(1)}) all-reduce(f32[2]{0:T(128)S(1)} %copy-done.43, f32[2]{0:T(128)S(1)} %get-tuple-element.57), channel_id=1, replica_groups=mesh['sub'=64,'rhs'=4] {'sub'}, use_global_device_ids=true, to_apply=%region_21.24 | all-reduce | flops 4 | bytes 32 | tf_op jit(solution)/shard_map/psum | solution.py:100
  1279.7 2.6 collective-permute-start.11
  1282.2 5.4 fusion.63
  1288.6 10.5 multiply_reduce_fusion.5
  1299.1 123.0 %psum.145 = f32[2]{0:T(128)S(1)} all-reduce(f32[2]{0:T(128)S(1)} %get-tuple-element.59), channel_id=1, replica_groups=mesh['sub'=64,'rhs'=4] {'sub'}, use_global_device_ids=true, to_apply=%region_25.28 | all-reduce | flops 2 | bytes 16 | tf_op jit(solution)/shard_map/psum | solution.py:100
  1422.2 3.8 convolution_bitcast_fusion.12
  1426.0 2.2 multiply_reduce_fusion.3
  1428.2 5.2 fusion.66
  1433.5 125.2 %all-reduce.1 = (f32[2]{0:T(128)S(1)}, f32[2]{0:T(128)S(1)}) all-reduce(f32[2]{0:T(128)S(1)} %copy-done.42, f32[2]{0:T(128)S(1)} %get-tuple-element.61), channel_id=1, replica_groups=mesh['sub'=64,'rhs'=4] {'sub'}, use_global_device_ids=true, to_apply=%region_27.30 | all-reduce | flops 4 | bytes 32 | tf_op jit(solution)/shard_map/psum | solution.py:100
  1559.4 1.9 collective-permute-start.12
  1561.3 2.7 collective-permute-start.13
  1564.0 5.3 fusion.65
  1570.2 10.5 multiply_reduce_fusion.2
  1580.7 123.3 %psum.148 = f32[2]{0:T(128)S(1)} all-reduce(f32[2]{0:T(128)S(1)} %get-tuple-element.63), channel_id=1, replica_groups=mesh['sub'=64,'rhs'=4] {'sub'}, use_global_device_ids=true, to_apply=%region_31.34 | all-reduce | flops 2 | bytes 16 | tf_op jit(solution)/shard_map/psum | solution.py:100
  1704.1 3.8 convolution_bitcast_fusion.10
  1707.9 2.2 multiply_reduce_fusion
  1710.1 5.2 fusion.68
  1715.4 125.2 %all-reduce = (f32[2]{0:T(128)S(1)}, f32[2]{0:T(128)S(1)}) all-reduce(f32[2]{0:T(128)S(1)} %copy-done.41, f32[2]{0:T(128)S(1)} %get-tuple-element.65), channel_id=1, replica_groups=mesh['sub'=64,'rhs'=4] {'sub'}, use_global_device_ids=true, to_apply=%region_33.36 | all-reduce | flops 4 | bytes 32 | tf_op jit(solution)/shard_map/psum | solution.py:100
  1841.3 1.9 collective-permute-start.14
  1843.3 2.6 collective-permute-start.15
  1845.9 5.3 fusion.67
  1852.1 10.8 fusion.1
  1862.9 3.8 convolution_bitcast_fusion.8
  1866.7 3.9 fusion.69
  1870.6 4.3 add_add_fusion
  1874.9 2.5 reshape.57
  1878.2 106.4 %all-reduce.7.cloned.1.call-done = f32[48,9216]{1,0:T(8,128)} async-done(((f32[48,9216]{1,0:T(8,128)}), f32[48,9216]{1,0:T(8,128)}) %all-reduce.7.cloned.1.call-update) | async-done | bytes 1769488 | tf_op jit(solution)/shard_map/psum | solution.py:125
  1984.6 2.8 copy.72
  (192 shorter events, 26.9 us)
Async XLA Ops:
  7.2 1977.4 %all-reduce.7.cloned.1.call-start = ((), (), s32[]{:S(2)}) async-start(), calls=%async_computation | async-start | bytes 3538944 | tf_op jit(solution)/shard_map/psum | solution.py:125
  12.3 13.1 copy-start.13
  18.9 17.5 collective-permute-start
  23.5 12.9 collective-permute-start.1
  175.6 6.1 copy-start.44
  175.6 133.5 %copy-start.19 = (f32[2]{0:T(128)}, f32[2]{0:T(128)S(1)}, u32[]{:S(2)}) copy-start(f32[2]{0:T(128)S(1)} %get-tuple-element.19) | copy-start | bytes 28
  179.5 148.7 %copy-start.6 = (f32[2,48,96]{2,0,1:T(2,128)}, f32[2,48,96]{2,0,1:T(2,128)S(1)}, u32[]{:S(2)}) copy-start(f32[2,48,96]{2,0,1:T(2,128)S(1)} %convolution_bitcast_fusion.20) | copy-start | bytes 110596
  309.1 0.7 copy-start.14
  309.9 4.3 collective-permute-start.2
  311.8 4.9 collective-permute-start.3
  450.4 6.1 copy-start.21
  454.2 128.2 %copy-start.8 = (f32[2,48,96]{2,0,1:T(2,128)}, f32[2,48,96]{2,0,1:T(2,128)S(1)}, u32[]{:S(2)}) copy-start(f32[2,48,96]{2,0,1:T(2,128)S(1)} %convolution_bitcast_fusion.18) | copy-start | bytes 110596
  582.4 19.0 copy-start.16
  583.2 4.3 collective-permute-start.4
  585.1 4.9 collective-permute-start.5
  723.7 6.1 copy-start.24
  723.8 137.1 %copy-start.12 = (f32[2,4608]{1,0:T(2,128)S(1)}, f32[2,4608]{1,0:T(2,128)}, u32[]{:S(2)}) copy-start(f32[2,4608]{1,0:T(2,128)} %param.14) | copy-start | bytes 110596
  727.6 130.9 %copy-start.10 = (f32[2,48,96]{2,0,1:T(2,128)}, f32[2,48,96]{2,0,1:T(2,128)S(1)}, u32[]{:S(2)}) copy-start(f32[2,48,96]{2,0,1:T(2,128)S(1)} %convolution_bitcast_fusion.16) | copy-start | bytes 110596
  855.8 141.7 %copy-start.27 = (f32[2]{0:T(128)}, f32[2]{0:T(128)S(1)}, u32[]{:S(2)}) copy-start(f32[2]{0:T(128)S(1)} %psum.139) | copy-start | bytes 28
  855.8 19.7 copy-start.18
  856.5 4.5 collective-permute-start.6
  858.5 4.9 collective-permute-start.7
  997.4 0.6 copy-start.37
  997.5 0.6 copy-start.39
  998.8 6.2 collective-permute-start.8
  1000.7 4.9 collective-permute-start.9
  1006.6 134.0 %copy-start.38 = (f32[2]{0:T(128)S(1)}, f32[2]{0:T(128)}, u32[]{:S(2)}) copy-start(f32[2]{0:T(128)} %copy-done.37) | copy-start | bytes 28
  1006.6 133.9 %copy-start.40 = (f32[2]{0:T(128)S(1)}, f32[2]{0:T(128)}, u32[]{:S(2)}) copy-start(f32[2]{0:T(128)} %copy-done.39) | copy-start | bytes 28
  1140.5 6.1 copy-start.31
  1144.4 7.5 copy-start.43
  1144.4 132.0 %copy-start.25 = (f32[2]{0:T(128)S(1)}, f32[2]{0:T(128)}, u32[]{:S(2)}) copy-start(f32[2]{0:T(128)} %copy-done.24) | copy-start | bytes 28
  1144.4 137.8 %copy-start.11 = (f32[2,48,96]{2,0,1:T(2,128)S(1)}, f32[2,48,96]{2,0,1:T(2,128)}, u32[]{:S(2)}) copy-start(f32[2,48,96]{2,0,1:T(2,128)} %copy-done.10) | copy-start | bytes 110596
  1276.4 0.5 copy-start.33
  1276.4 0.6 copy-start.35
  1277.7 9.9 collective-permute-start.10
  1279.7 8.0 collective-permute-start.11
  1288.5 133.6 %copy-start.26 = (f32[2]{0:T(128)S(1)}, f32[2]{0:T(128)}, u32[]{:S(2)}) copy-start(f32[2]{0:T(128)} %copy-done.24) | copy-start | bytes 28
  1288.5 133.6 %copy-start.28 = (f32[2]{0:T(128)S(1)}, f32[2]{0:T(128)}, u32[]{:S(2)}) copy-start(f32[2]{0:T(128)} %copy-done.27) | copy-start | bytes 28
  1288.5 133.5 %copy-start.32 = (f32[2]{0:T(128)S(1)}, f32[2]{0:T(128)}, u32[]{:S(2)}) copy-start(f32[2]{0:T(128)} %copy-done.31) | copy-start | bytes 28
  1288.5 133.5 %copy-start.34 = (f32[2]{0:T(128)S(1)}, f32[2]{0:T(128)}, u32[]{:S(2)}) copy-start(f32[2]{0:T(128)} %copy-done.33) | copy-start | bytes 28
  1288.5 133.5 %copy-start.36 = (f32[2]{0:T(128)S(1)}, f32[2]{0:T(128)}, u32[]{:S(2)}) copy-start(f32[2]{0:T(128)} %copy-done.35) | copy-start | bytes 28
  1422.1 3.9 copy-start.29
  1426.0 7.5 copy-start.42
  1426.0 132.6 %copy-start.22 = (f32[2]{0:T(128)S(1)}, f32[2]{0:T(128)}, u32[]{:S(2)}) copy-start(f32[2]{0:T(128)} %copy-done.21) | copy-start | bytes 28
  1426.0 138.0 %copy-start.9 = (f32[2,48,96]{2,0,1:T(2,128)S(1)}, f32[2,48,96]{2,0,1:T(2,128)}, u32[]{:S(2)}) copy-start(f32[2,48,96]{2,0,1:T(2,128)} %copy-done.8) | copy-start | bytes 110596
  1428.2 142.0 %copy-start.17 = (f32[2]{0:T(128)S(1)}, f32[2]{0:T(128)}, u32[]{:S(2)}) copy-start(f32[2]{0:T(128)} %copy-done.16) | copy-start | bytes 28
  1559.4 9.9 collective-permute-start.12
  1561.3 8.0 collective-permute-start.13
  1570.2 133.8 %copy-start.20 = (f32[2]{0:T(128)S(1)}, f32[2]{0:T(128)}, u32[]{:S(2)}) copy-start(f32[2]{0:T(128)} %copy-done.19) | copy-start | bytes 28
  1570.2 133.8 %copy-start.23 = (f32[2]{0:T(128)S(1)}, f32[2]{0:T(128)}, u32[]{:S(2)}) copy-start(f32[2]{0:T(128)} %copy-done.21) | copy-start | bytes 28
  1570.2 133.8 %copy-start.30 = (f32[2]{0:T(128)S(1)}, f32[2]{0:T(128)}, u32[]{:S(2)}) copy-start(f32[2]{0:T(128)} %copy-done.29) | copy-start | bytes 28
  1707.9 7.5 copy-start.41
  1707.9 132.6 %copy-start.45 = (f32[2]{0:T(128)S(1)}, f32[2]{0:T(128)}, u32[]{:S(2)}) copy-start(f32[2]{0:T(128)} %copy-done.44) | copy-start | bytes 28
  1707.9 138.0 %copy-start.7 = (f32[2,48,96]{2,0,1:T(2,128)S(1)}, f32[2,48,96]{2,0,1:T(2,128)}, u32[]{:S(2)}) copy-start(f32[2,48,96]{2,0,1:T(2,128)} %copy-done.6) | copy-start | bytes 110596
  1710.1 142.0 %copy-start.15 = (f32[2]{0:T(128)S(1)}, f32[2]{0:T(128)}, u32[]{:S(2)}) copy-start(f32[2]{0:T(128)} %copy-done.14) | copy-start | bytes 28
  1841.3 9.8 collective-permute-start.14
  1843.3 7.9 collective-permute-start.15
  1852.1 18.4 copy-start.2
  1852.1 18.4 copy-start.3
  1852.1 18.4 copy-start.4
  1852.1 18.4 copy-start.5
  1862.9 7.7 copy-start
  1862.9 7.7 copy-start.1
Sparse Core Ops, SparseCore 0:
  1877.6 106.9 all-reduce.6
where the time goes:
time: 2000 us; the launch traced here: 1990 us
  blocking collectives  1620 us (81%)
  matrix products  170 us (8%)
  waiting for transfers between devices  115 us (6%)
  starting transfers between devices  39.2 us (2%)
  local copies, waits for them, and re-layouts  32.9 us (2%)
    psum x6, blocking collectives, shards(): lax.psum((local_dot(dir_bar, direction), local_dot(target, direction)), '...  745 us
    psum x4, blocking collectives, norm_sum(): return lax.psum(local_dot(first_vec, second_vec), 'sub')  507 us
    psum x3, blocking collectives, shards(): curvature = lax.psum(local_dot(direction, applied), 'sub')  366 us
    psum x1, waiting for transfers between devices, shards(): grad_sum = lax.psum(grad_sum, 'rhs')  106 us
    dot_general x8, matrix products, block_product(): return jnp.einsum('nkab,rnkb->rna', blocks, gathered, precision=highest)  84.9 us
  transfers between devices with their start and end apart: 17, of which 5 were waited for; matrix products, arithmetic and copies ran while one was open for 1% of the time, Pallas kernels for 0%

commit v1 on v0

--- a/solution.py
+++ b/solution.py
@@ -122,7 +122,11 @@
     zeta_bar = dir_bar + widen(norm_bar) * first_res
     weight_zeta = jnp.einsum("nab,rnb->rna", weights, zeta_bar, precision=highest)
     grad_sum = grad_sum + grad_term(first_proj, zeta_bar, weight_zeta, first_res)
-    grad_sum = lax.psum(grad_sum, "rhs")
+    devices, result = (lax.axis_size("rhs"), grad_sum)
+    for hop in [1 << k for k in range(devices.bit_length() - 1)]:
+        route = [(i_2, i_2 ^ hop) for i_2 in range(devices)]
+        result = result + lax.ppermute(result, "rhs", route)
+    grad_sum = result
     flat_solution = solution.reshape(local_rhs, NBLK * BS)
     return (flat_solution, grad_sum.reshape(NBLK, BS * BS))
 

time: 2000 us -> 2030 us (1.015)
  the two profiles are of different devices: /device:TPU:1 before, /device:TPU:128 now
where the time goes in v1:
time: 2030 us; the launch traced here: 2020 us
  blocking collectives  1640 us (81%)
  matrix products  170 us (8%)
  waiting for transfers between devices  99.5 us (5%)
  starting transfers between devices  77.8 us (4%)
  local copies, waits for them, and re-layouts  31.1 us (2%)
    psum x6, blocking collectives, shards(): lax.psum((local_dot(dir_bar, direction), local_dot(target, direction)), '...  752 us
    psum x4, blocking collectives, norm_sum(): return lax.psum(local_dot(first_vec, second_vec), 'sub')  497 us
    psum x3, blocking collectives, shards(): curvature = lax.psum(local_dot(direction, applied), 'sub')  388 us
    ppermute x2, waiting for transfers between devices, shards(): result = result + lax.ppermute(result, 'rhs', route)  94.7 us
    dot_general x8, matrix products, block_product(): return jnp.einsum('nkab,rnkb->rna', blocks, gathered, precision=highest)  84.9 us
    ppermute x8, starting transfers between devices, with_halo(): after = lax.ppermute(initial, axis, down)  56.7 us
  transfers between devices with their start and end apart: 18, of which 6 were waited for; matrix products, arithmetic and copies ran while one was open for 1% of the time, Pallas kernels for 0%

profile of v1, /device:TPU:128, one launch (start us, length us, event | category | flops | bytes accessed | tf_op | source)
XLA Modules:
  0.0 2024.1 jit_solution(12514923845285997829)
XLA Ops:
  3.5 2.2 reshape.53
  5.8 3.8 convolution_bitcast_fusion.22
  9.6 2.1 fusion.14
  12.3 1.9 collective-permute-start
  14.3 7.0 collective-permute-start.1
  21.6 10.6 reshape.54
  33.1 10.6 multiply_reduce_fusion.16
  43.6 124.5 %all-reduce.4 = (f32[2]{0:T(128)S(1)}, f32[2]{0:T(128)S(1)}) all-reduce(f32[2]{0:T(128)S(1)} %get-tuple-element.10, f32[2]{0:T(128)S(1)} %get-tuple-element.9), channel_id=1, replica_groups=mesh['sub'=64,'rhs'=4] {'sub'}, use_global_device_ids=true, to_apply=%region_1.0 | all-reduce | flops 4 | bytes 32 | tf_op jit(solution)/shard_map/psum | solution.py:52
  168.3 3.8 convolution_bitcast_fusion.20
  172.0 2.2 multiply_reduce_fusion.15
  174.3 124.1 %psum.128 = f32[2]{0:T(128)S(1)} all-reduce(f32[2]{0:T(128)S(1)} %get-tuple-element.44), channel_id=1, replica_groups=mesh['sub'=64,'rhs'=4] {'sub'}, use_global_device_ids=true, to_apply=%region_5.8 | all-reduce | flops 2 | bytes 16 | tf_op jit(solution)/shard_map/psum | solution.py:52
  299.1 1.9 collective-permute-start.2
  301.1 7.0 collective-permute-start.3
  310.3 10.5 multiply_reduce_fusion.14
  320.8 129.2 %psum.129 = f32[2]{0:T(128)S(1)} all-reduce(f32[2]{0:T(128)S(1)} %get-tuple-element.46), channel_id=1, replica_groups=mesh['sub'=64,'rhs'=4] {'sub'}, use_global_device_ids=true, to_apply=%region_7.10 | all-reduce | flops 2 | bytes 16 | tf_op jit(solution)/shard_map/psum | solution.py:79
  450.1 3.8 convolution_bitcast_fusion.18
  453.9 2.2 multiply_reduce_fusion.13
  456.1 124.1 %psum.130 = f32[2]{0:T(128)S(1)} all-reduce(f32[2]{0:T(128)S(1)} %get-tuple-element.48), channel_id=1, replica_groups=mesh['sub'=64,'rhs'=4] {'sub'}, use_global_device_ids=true, to_apply=%region_9.12 | all-reduce | flops 2 | bytes 16 | tf_op jit(solution)/shard_map/psum | solution.py:52
  580.9 1.9 collective-permute-start.4
  582.9 7.0 collective-permute-start.5
  592.1 10.5 multiply_reduce_fusion.12
  602.6 129.3 %psum.131 = f32[2]{0:T(128)S(1)} all-reduce(f32[2]{0:T(128)S(1)} %get-tuple-element.50), channel_id=1, replica_groups=mesh['sub'=64,'rhs'=4] {'sub'}, use_global_device_ids=true, to_apply=%region_11.14 | all-reduce | flops 2 | bytes 16 | tf_op jit(solution)/shard_map/psum | solution.py:79
  732.0 3.8 convolution_bitcast_fusion.16
  735.7 2.2 multiply_reduce_fusion.11
  738.0 124.1 %psum.132 = f32[2]{0:T(128)S(1)} all-reduce(f32[2]{0:T(128)S(1)} %get-tuple-element.52), channel_id=1, replica_groups=mesh['sub'=64,'rhs'=4] {'sub'}, use_global_device_ids=true, to_apply=%region_13.16 | all-reduce | flops 2 | bytes 16 | tf_op jit(solution)/shard_map/psum | solution.py:52
  864.8 7.0 collective-permute-start.7
  874.0 11.1 multiply_reduce_fusion.1
  885.0 129.1 %all-reduce.3 = (f32[2]{0:T(128)S(1)}, f32[2]{0:T(128)S(1)}) all-reduce(f32[2]{0:T(128)S(1)} %get-tuple-element.6, f32[2]{0:T(128)S(1)} %get-tuple-element.5), channel_id=1, replica_groups=mesh['sub'=64,'rhs'=4] {'sub'}, use_global_device_ids=true, to_apply=%region_15.18 | all-reduce | flops 4 | bytes 32 | tf_op jit(solution)/shard_map/psum | solution.py:79
  1015.4 1.9 collective-permute-start.8
  1017.3 7.4 collective-permute-start.9
  1026.5 10.5 multiply_reduce_fusion.8
  1037.0 129.1 %psum.135 = f32[2]{0:T(128)S(1)} all-reduce(f32[2]{0:T(128)S(1)} %get-tuple-element.55), channel_id=1, replica_groups=mesh['sub'=64,'rhs'=4] {'sub'}, use_global_device_ids=true, to_apply=%region_19.22 | all-reduce | flops 2 | bytes 16 | tf_op jit(solution)/shard_map/psum | solution.py:100
  1166.2 3.8 convolution_bitcast_fusion.14
  1170.0 2.2 multiply_reduce_fusion.6
  1172.2 5.2 fusion.64
  1177.4 124.0 %all-reduce.2 = (f32[2]{0:T(128)S(1)}, f32[2]{0:T(128)S(1)}) all-reduce(f32[2]{0:T(128)S(1)} %copy-done.43, f32[2]{0:T(128)S(1)} %get-tuple-element.57), channel_id=1, replica_groups=mesh['sub'=64,'rhs'=4] {'sub'}, use_global_device_ids=true, to_apply=%region_21.24 | all-reduce | flops 4 | bytes 32 | tf_op jit(solution)/shard_map/psum | solution.py:100
  1302.8 1.9 collective-permute-start.10
  1304.7 7.1 collective-permute-start.11
  1311.9 5.4 fusion.63
  1318.2 10.5 multiply_reduce_fusion.5
  1328.7 125.1 %psum.138 = f32[2]{0:T(128)S(1)} all-reduce(f32[2]{0:T(128)S(1)} %get-tuple-element.59), channel_id=1, replica_groups=mesh['sub'=64,'rhs'=4] {'sub'}, use_global_device_ids=true, to_apply=%region_25.28 | all-reduce | flops 2 | bytes 16 | tf_op jit(solution)/shard_map/psum | solution.py:100
  1453.9 3.8 convolution_bitcast_fusion.12
  1457.7 2.2 multiply_reduce_fusion.3
  1459.9 5.2 fusion.66
  1465.2 124.0 %all-reduce.1 = (f32[2]{0:T(128)S(1)}, f32[2]{0:T(128)S(1)}) all-reduce(f32[2]{0:T(128)S(1)} %copy-done.42, f32[2]{0:T(128)S(1)} %get-tuple-element.61), channel_id=1, replica_groups=mesh['sub'=64,'rhs'=4] {'sub'}, use_global_device_ids=true, to_apply=%region_27.30 | all-reduce | flops 4 | bytes 32 | tf_op jit(solution)/shard_map/psum | solution.py:100
  1591.9 7.2 collective-permute-start.13
  1599.2 5.3 fusion.65
  1605.4 10.5 multiply_reduce_fusion.2
  1615.9 125.3 %psum.141 = f32[2]{0:T(128)S(1)} all-reduce(f32[2]{0:T(128)S(1)} %get-tuple-element.63), channel_id=1, replica_groups=mesh['sub'=64,'rhs'=4] {'sub'}, use_global_device_ids=true, to_apply=%region_31.34 | all-reduce | flops 2 | bytes 16 | tf_op jit(solution)/shard_map/psum | solution.py:100
  1741.3 3.8 convolution_bitcast_fusion.10
  1745.1 2.2 multiply_reduce_fusion
  1747.3 5.3 fusion.68
  1752.6 124.0 %all-reduce = (f32[2]{0:T(128)S(1)}, f32[2]{0:T(128)S(1)}) all-reduce(f32[2]{0:T(128)S(1)} %copy-done.41, f32[2]{0:T(128)S(1)} %get-tuple-element.65), channel_id=1, replica_groups=mesh['sub'=64,'rhs'=4] {'sub'}, use_global_device_ids=true, to_apply=%region_33.36 | all-reduce | flops 4 | bytes 32 | tf_op jit(solution)/shard_map/psum | solution.py:100
  1879.4 7.1 collective-permute-start.15
  1886.6 5.3 fusion.67
  1892.8 10.8 fusion.1
  1903.6 3.8 convolution_bitcast_fusion.8
  1907.4 3.9 fusion.69
  1911.3 4.1 add_add_fusion
  1917.0 47.9 %collective-permute-done.16 = f32[48,96,96]{2,1,0:T(8,128)S(1)} collective-permute-done((f32[48,96,96]{2,1,0:T(8,128)S(1)}, f32[48,96,96]{2,1,0:T(8,128)S(1)}, u32[]{:S(2)}, u32[]{:S(2)}) %collective-permute-start.16) | collective-permute-done | bytes 1769504 | tf_op jit(solution)/shard_map/ppermute | solution.py:128
  1965.3 4.1 collective-permute-start.17
  1970.1 46.9 %collective-permute-done.17 = f32[48,96,96]{2,1,0:T(8,128)} collective-permute-done((f32[48,96,96]{2,1,0:T(8,128)S(1)}, f32[48,96,96]{2,1,0:T(8,128)}, u32[]{:S(2)}, u32[]{:S(2)}) %collective-permute-start.17) | collective-permute-done | bytes 1769504 | tf_op jit(solution)/shard_map/ppermute | solution.py:128
  2017.0 3.3 add.236
  2020.3 3.6 reshape.57
  (194 shorter events, 30.9 us)
Async XLA Ops:
  5.7 15.5 copy-start.13
  12.3 19.8 collective-permute-start
  14.3 17.9 collective-permute-start.1
  168.2 6.1 copy-start.44
  168.2 130.2 %copy-start.19 = (f32[2]{0:T(128)}, f32[2]{0:T(128)S(1)}, u32[]{:S(2)}) copy-start(f32[2]{0:T(128)S(1)} %get-tuple-element.19) | copy-start | bytes 28
  172.0 148.7 %copy-start.6 = (f32[2,48,96]{2,0,1:T(2,128)}, f32[2,48,96]{2,0,1:T(2,128)S(1)}, u32[]{:S(2)}) copy-start(f32[2,48,96]{2,0,1:T(2,128)S(1)} %convolution_bitcast_fusion.20) | copy-start | bytes 110596
  298.3 0.7 copy-start.14
  299.1 8.9 collective-permute-start.2
  301.1 8.3 collective-permute-start.3
  450.0 6.1 copy-start.21
  453.9 148.7 %copy-start.8 = (f32[2,48,96]{2,0,1:T(2,128)}, f32[2,48,96]{2,0,1:T(2,128)S(1)}, u32[]{:S(2)}) copy-start(f32[2,48,96]{2,0,1:T(2,128)S(1)} %convolution_bitcast_fusion.18) | copy-start | bytes 110596
  580.2 22.4 %copy-start.16 = (f32[2]{0:T(128)}, f32[2]{0:T(128)S(1)}, u32[]{:S(2)}) copy-start(f32[2]{0:T(128)S(1)} %div.66) | copy-start | bytes 28
  580.9 8.9 collective-permute-start.4
  582.9 8.3 collective-permute-start.5
  731.9 6.1 copy-start.24
  732.0 139.7 %copy-start.12 = (f32[2,4608]{1,0:T(2,128)S(1)}, f32[2,4608]{1,0:T(2,128)}, u32[]{:S(2)}) copy-start(f32[2,4608]{1,0:T(2,128)} %param.14) | copy-start | bytes 110596
  735.7 129.0 %copy-start.10 = (f32[2,48,96]{2,0,1:T(2,128)}, f32[2,48,96]{2,0,1:T(2,128)S(1)}, u32[]{:S(2)}) copy-start(f32[2,48,96]{2,0,1:T(2,128)S(1)} %convolution_bitcast_fusion.16) | copy-start | bytes 110596
  862.0 152.1 %copy-start.27 = (f32[2]{0:T(128)}, f32[2]{0:T(128)S(1)}, u32[]{:S(2)}) copy-start(f32[2]{0:T(128)S(1)} %psum.132) | copy-start | bytes 28
  862.0 23.0 %copy-start.18 = (f32[2]{0:T(128)}, f32[2]{0:T(128)S(1)}, u32[]{:S(2)}) copy-start(f32[2]{0:T(128)S(1)} %div.68) | copy-start | bytes 28
  862.8 9.0 collective-permute-start.6
  864.8 8.3 collective-permute-start.7
  1014.1 0.5 copy-start.37
  1014.1 0.5 copy-start.39
  1015.4 9.3 collective-permute-start.8
  1017.3 8.3 collective-permute-start.9
  1026.5 139.6 %copy-start.38 = (f32[2]{0:T(128)S(1)}, f32[2]{0:T(128)}, u32[]{:S(2)}) copy-start(f32[2]{0:T(128)} %copy-done.37) | copy-start | bytes 28
  1026.5 139.6 %copy-start.40 = (f32[2]{0:T(128)S(1)}, f32[2]{0:T(128)}, u32[]{:S(2)}) copy-start(f32[2]{0:T(128)} %copy-done.39) | copy-start | bytes 28
  1166.1 6.1 copy-start.31
  1170.0 7.5 copy-start.43
  1170.0 131.5 %copy-start.25 = (f32[2]{0:T(128)S(1)}, f32[2]{0:T(128)}, u32[]{:S(2)}) copy-start(f32[2]{0:T(128)} %copy-done.24) | copy-start | bytes 28
  1170.0 141.9 %copy-start.11 = (f32[2,48,96]{2,0,1:T(2,128)S(1)}, f32[2,48,96]{2,0,1:T(2,128)}, u32[]{:S(2)}) copy-start(f32[2,48,96]{2,0,1:T(2,128)} %copy-done.10) | copy-start | bytes 110596
  1301.5 0.6 copy-start.33
  1301.5 0.6 copy-start.35
  1302.8 14.4 collective-permute-start.10
  1304.7 12.5 collective-permute-start.11
  1318.2 135.6 %copy-start.26 = (f32[2]{0:T(128)S(1)}, f32[2]{0:T(128)}, u32[]{:S(2)}) copy-start(f32[2]{0:T(128)} %copy-done.24) | copy-start | bytes 28
  1318.2 135.6 %copy-start.28 = (f32[2]{0:T(128)S(1)}, f32[2]{0:T(128)}, u32[]{:S(2)}) copy-start(f32[2]{0:T(128)} %copy-done.27) | copy-start | bytes 28
  1318.2 135.6 %copy-start.32 = (f32[2]{0:T(128)S(1)}, f32[2]{0:T(128)}, u32[]{:S(2)}) copy-start(f32[2]{0:T(128)} %copy-done.31) | copy-start | bytes 28
  1318.2 135.6 %copy-start.34 = (f32[2]{0:T(128)S(1)}, f32[2]{0:T(128)}, u32[]{:S(2)}) copy-start(f32[2]{0:T(128)} %copy-done.33) | copy-start | bytes 28
  1318.2 135.6 %copy-start.36 = (f32[2]{0:T(128)S(1)}, f32[2]{0:T(128)}, u32[]{:S(2)}) copy-start(f32[2]{0:T(128)} %copy-done.35) | copy-start | bytes 28
  1453.8 3.9 copy-start.29
  1457.7 7.5 copy-start.42
  1457.7 131.5 %copy-start.22 = (f32[2]{0:T(128)S(1)}, f32[2]{0:T(128)}, u32[]{:S(2)}) copy-start(f32[2]{0:T(128)} %copy-done.21) | copy-start | bytes 28
  1457.7 141.5 %copy-start.9 = (f32[2,48,96]{2,0,1:T(2,128)S(1)}, f32[2,48,96]{2,0,1:T(2,128)}, u32[]{:S(2)}) copy-start(f32[2,48,96]{2,0,1:T(2,128)} %copy-done.8) | copy-start | bytes 110596
  1459.9 145.4 %copy-start.17 = (f32[2]{0:T(128)S(1)}, f32[2]{0:T(128)}, u32[]{:S(2)}) copy-start(f32[2]{0:T(128)} %copy-done.16) | copy-start | bytes 28
  1590.0 14.4 collective-permute-start.12
  1591.9 12.5 collective-permute-start.13
  1605.4 135.9 %copy-start.20 = (f32[2]{0:T(128)S(1)}, f32[2]{0:T(128)}, u32[]{:S(2)}) copy-start(f32[2]{0:T(128)} %copy-done.19) | copy-start | bytes 28
  1605.4 135.9 %copy-start.23 = (f32[2]{0:T(128)S(1)}, f32[2]{0:T(128)}, u32[]{:S(2)}) copy-start(f32[2]{0:T(128)} %copy-done.21) | copy-start | bytes 28
  1605.4 135.8 %copy-start.30 = (f32[2]{0:T(128)S(1)}, f32[2]{0:T(128)}, u32[]{:S(2)}) copy-start(f32[2]{0:T(128)} %copy-done.29) | copy-start | bytes 28
  1745.1 7.5 copy-start.41
  1745.1 131.5 %copy-start.45 = (f32[2]{0:T(128)S(1)}, f32[2]{0:T(128)}, u32[]{:S(2)}) copy-start(f32[2]{0:T(128)} %copy-done.44) | copy-start | bytes 28
  1745.1 141.4 %copy-start.7 = (f32[2,48,96]{2,0,1:T(2,128)S(1)}, f32[2,48,96]{2,0,1:T(2,128)}, u32[]{:S(2)}) copy-start(f32[2,48,96]{2,0,1:T(2,128)} %copy-done.6) | copy-start | bytes 110596
  1747.3 145.4 %copy-start.15 = (f32[2]{0:T(128)S(1)}, f32[2]{0:T(128)}, u32[]{:S(2)}) copy-start(f32[2]{0:T(128)} %copy-done.14) | copy-start | bytes 28
  1877.5 14.4 collective-permute-start.14
  1879.4 12.4 collective-permute-start.15
  1892.8 18.4 copy-start.2
  1892.8 18.4 copy-start.3
  1892.8 18.4 copy-start.4
  1892.8 18.4 copy-start.5
  1903.6 7.7 copy-start
  1903.6 7.7 copy-start.1
  1915.4 49.4 %collective-permute-start.16 = (f32[48,96,96]{2,1,0:T(8,128)S(1)}, f32[48,96,96]{2,1,0:T(8,128)S(1)}, u32[]{:S(2)}, u32[]{:S(2)}) collective-permute-start(f32[48,96,96]{2,1,0:T(8,128)S(1)} %add_add_fusion), channel_id=1, source_target_pairs={{0,1},{1,0},{2,3},{3,2},{4,5},{5,4},{6,7},{7,6},{8,9},{9,8},{10,11... | collective-permute-start | bytes 5308424 | tf_op jit(solution)/shard_map/ppermute | solution.py:128
  1965.3 51.7 %collective-permute-start.17 = (f32[48,96,96]{2,1,0:T(8,128)S(1)}, f32[48,96,96]{2,1,0:T(8,128)}, u32[]{:S(2)}, u32[]{:S(2)}) collective-permute-start(f32[48,96,96]{2,1,0:T(8,128)S(1)} %add.235), channel_id=1, source_target_pairs={{0,2},{1,3},{2,0},{3,1},{4,6},{5,7},{6,4},{7,5},{8,10},{9,11},{10,... | collective-permute-start | bytes 5308424 | tf_op jit(solution)/shard_map/ppermute | solution.py:128
